TPU v7x, 32 devices: a whole 2x2x4 slice. The times are simulated.
32 devices in a mesh: inst: 4 (over x, core), lab: 8 (over z, y).
Axes of the slice: x: 2, y: 2, z: 4, core: 2. Of those that a mesh axis runs over, the one named last changes fastest.
Arguments:
- features: bfloat16 [2048, 768], P('inst'), may hold values from -6 to 6
- tile_rows: int32 [128], P(('inst', 'lab')), may hold values from 0 to 1, as said below
- tile_labels: int32 [128], P(('inst', 'lab')), may hold values from 0 to 3
- tile_values: bfloat16 [128, 256, 256], P(('inst', 'lab')), may hold values from 0 to 1
- cluster_ids: int32 [8192], P(('lab', 'inst')), may hold values from 0 to 1023, as said below
Outputs:
- label_embed: float32 [8192, 768], P(('lab', 'inst'))
- centroids: float32 [1024, 768], P(('inst', 'lab'))
Inputs may be any that keep to these rules, and one draw needn't show every extreme that they name: Within each block of 4 entries the pairs (tile_rows, tile_labels) are distinct. Within each aligned block of 256 labels, at most 16 labels have clusters with the same value of cluster_ids // 32, and that many is reached in every block.
All inputs are finite; a program needn't handle non-finite values.
Results may differ from a plain program's by a relative error of at most 0.01.
Values may be sent and summed in bfloat16 or wider, within the bound.
A program may use at most 128 MiB of HBM per device.

v0:
```python
import functools

import jax
import jax.numpy as jnp
from jax import lax
from jax.experimental import pallas as pl
from jax.experimental.pallas import tpu as pltpu
from jax.sharding import PartitionSpec as P

CL_OWN = 32
PAIR = 2
LAG = 3
MESH = pl.DeviceIdType.MESH


def unit_rows(matrix):
    return matrix * lax.rsqrt(jnp.sum(matrix * matrix, axis=-1, keepdims=True) + 1e-06)


def segments(tile):
    part = tile // 8
    tail = part // 2
    return [(q * part, part) for q in range(7)] + [(7 * part, tail), (7 * part + tail, tail)]


def blocks(tile):
    return [(0, tile // 2), (tile // 2, 3 * tile // 4), (3 * tile // 4, tile)]


def kernel(
    nx, ny, nz,
    rows_hbm, labs_hbm, ids_hbm, feat_hbm, val_hbm,
    emb_ref, cen_ref,
    rows_s, labs_s, feat, vals, xn, vt, csend, crecv, xsend, xrecv, total,
    eb, ids, picks0, picks1, picks2, acc,
    sa, ra, oa, sb, rb, ob, ya_s, ya_r, fa, xb_s, xb_r, fb, z_s, z_r,
    m_in, m_val, m_feat,
    s_core, r_core, s_x, r_x, s_zg, r_zg, s_cg, r_cg, s_fw, r_fw, s_ids, r_ids,
    s_sa, r_sa, s_sb, r_sb, s_ya, r_ya, s_xb, r_xb, s_za, r_za, s_zb, r_zb,
):
    inst = lax.axis_index("inst")
    lab = lax.axis_index("lab")
    x, c = inst // 2, inst % 2
    z, y = lab // ny, lab % ny
    other = 1 - c
    n_tiles, tile = val_hbm.shape[0], val_hbm.shape[1]
    width = feat_hbm.shape[1]
    half = width // 2
    row_tiles = feat_hbm.shape[0] // tile
    segs = segments(tile)
    cuts = blocks(tile)
    n_seg = len(segs)

    x_at = lambda d: (x + d) % nx
    y_at = lambda d: (y + d) % ny
    zq, zr = z // PAIR, z % PAIR
    nq = nz // PAIR
    zq_at = lambda d: (zq + d) % nq
    core_peer = (x * 2 + other, lab)
    x_peer = lambda d: (x_at(d) * 2 + c, lab)
    y_peer = lambda d: (inst, z * ny + y_at(d))
    z_peer = lambda d: (inst, (zq_at(d) * PAIR + zr) * ny + y)
    pair_peer = (inst, (zq * PAIR + (PAIR - 1 - zr)) * ny + y)
    peers = [core_peer]
    peers += [x_peer(d) for d in range(1, nx)]
    peers += [y_peer(d) for d in range(1, ny)]
    peers += [z_peer(d) for d in range(1, nq)]
    peers.append(pair_peer)

    barrier = pltpu.get_barrier_semaphore()
    for peer in peers:
        pl.semaphore_signal(barrier, inc=1, device_id=peer, device_id_type=MESH)

    loads = [
        pltpu.make_async_copy(rows_hbm, rows_s, m_in.at[0]),
        pltpu.make_async_copy(labs_hbm, labs_s, m_in.at[1]),
    ]
    val_loads = [
        pltpu.make_async_copy(val_hbm.at[n], vals.at[n], m_val.at[n]) for n in range(n_tiles)
    ]
    feat_loads = [
        pltpu.make_async_copy(
            feat_hbm.at[pl.ds(r * tile, tile)], feat.at[pl.ds(r * tile, tile)], m_feat.at[r]
        )
        for r in range(row_tiles)
    ]
    ids_load = pltpu.make_async_copy(ids_hbm, ids.at[0], m_in.at[2])
    for copy in [*loads, *val_loads, *feat_loads, ids_load]:
        copy.start()

    def remote(src, dst, send, recv, peer):
        return pltpu.make_async_remote_copy(
            src_ref=src, dst_ref=dst, send_sem=send, recv_sem=recv,
            device_id=peer, device_id_type=MESH,
        )

    sent = []

    def go(copy):
        copy.start()
        sent.append(copy)
        return copy

    vt[n_tiles] = jnp.zeros((tile, tile), jnp.bfloat16)
    with jax.named_scope("A_wval"):
        for n in range(n_tiles):
            val_loads[n].wait()
            vt[n] = vals[n].T
    with jax.named_scope("B_wfeat"):
        for r in range(row_tiles):
            feat_loads[r].wait()
            rows = pl.ds(r * tile, tile)
            xn[rows] = unit_rows(feat[rows].astype(jnp.float32)).astype(jnp.bfloat16)
    for copy in loads:
        copy.wait()

    def partial(label_tile, rows):
        pieces = []
        for r in range(row_tiles):
            at = jnp.int32(n_tiles)
            for n in range(n_tiles):
                hit = jnp.logical_and(rows_s[n] == r, labs_s[n] == label_tile)
                at = jnp.where(hit, n, at)
            pieces.append(vt[at, rows])
        lhs = jnp.concatenate(pieces, axis=1)
        return jnp.dot(lhs, xn[...], preferred_element_type=jnp.float32)

    mid = tile // 2
    halves = [(0, mid), (mid, tile)]

    def core_copies(xp, low, high):
        return {
            q: remote(
                csend.at[xp, pl.ds(first, size)], crecv.at[xp, pl.ds(first, size)],
                s_core.at[xp, q], r_core.at[xp, q], core_peer,
            )
            for q, (first, size) in enumerate(segs)
            if low <= first < high
        }

    id_copies = [
        remote(ids.at[0], ids.at[1], s_ids.at[0], r_ids.at[0], core_peer),
        remote(ids.at[0], ids.at[2], s_ids.at[1], r_ids.at[1], pair_peer),
        remote(ids.at[2], ids.at[3], s_ids.at[2], r_ids.at[2], core_peer),
    ]
    x_copies = {}
    met = False
    for d in [*range(1, nx), 0]:
        xp = x_at(d)
        arriving = {}
        for low, high in halves:
            rows = pl.ds(low, high - low)
            with jax.named_scope("D_part%d" % d):
                csend[xp, rows] = partial(xp * 2 + other, rows).astype(jnp.bfloat16)
            if not met:
                met = True
                with jax.named_scope("C_barrier"):
                    pl.semaphore_wait(barrier, len(peers))
                ids_load.wait()
                go(id_copies[0])
                go(id_copies[1])
            for q, copy in core_copies(xp, low, high).items():
                arriving[q] = go(copy)
        with jax.named_scope("E_own%d" % d):
            total[...] = partial(xp * 2 + c, pl.ds(0, tile))
        for q, (first, size) in enumerate(segs):
            rows = pl.ds(first, size)
            with jax.named_scope("F_w%d_%d" % (d, q)):
                arriving[q].wait_recv()
            mixed = total[rows] + crecv[xp, rows].astype(jnp.float32)
            if d:
                xsend[d - 1, rows] = mixed.astype(jnp.bfloat16)
                x_copies[d, q] = go(
                    remote(
                        xsend.at[d - 1, rows], xrecv.at[d - 1, rows],
                        s_x.at[d - 1, q], r_x.at[d - 1, q], x_peer(d),
                    )
                )
            else:
                total[rows] = mixed

    def mark(picks, low, high):
        near = jnp.concatenate([ids[s, :, low:high] for s in range(2 * PAIR)], axis=1)
        count = 2 * PAIR * (high - low)
        near = jnp.broadcast_to(near, (CL_OWN, count))
        step = lax.broadcasted_iota(jnp.int32, (CL_OWN, count), 0)
        row = 0
        for dz in range(nq):
            for dx in range(nx):
                for dy in range(ny):
                    owner = (x_at(dx) * 2 + c) * nz + zq_at(dz) * PAIR + zr
                    base = (owner * ny + y_at(dy)) * CL_OWN
                    hit = jnp.where(near == step + base, 1.0, 0.0)
                    picks[pl.ds(row, CL_OWN)] = hit.astype(jnp.bfloat16)
                    row += CL_OWN

    pair_rows, core_rows, passed = {}, {}, {}

    def fetch(q):
        rows = pl.ds(*segs[q])
        with jax.named_scope("I_fetch%d" % q):
            pair_rows[q].wait_recv()
        passed[q] = go(
            remote(eb.at[2, rows], eb.at[3, rows], s_fw.at[q], r_fw.at[q], core_peer)
        )

    def gathered(cut):
        for q, (first, _) in enumerate(segs):
            if cut[0] <= first < cut[1]:
                core_rows[q].wait_recv()
                passed[q].wait_recv()
        return eb[:, cut[0] : cut[1]].reshape(2 * PAIR * (cut[1] - cut[0]), width)

    for q, (first, size) in enumerate(segs):
        rows = pl.ds(first, size)
        value = total[rows]
        with jax.named_scope("H_wx%d" % q):
            for d in range(1, nx):
                x_copies[d, q].wait_recv()
        for d in range(1, nx):
            value += xrecv[d - 1, rows].astype(jnp.float32)
        value = unit_rows(value)
        emb_ref[rows] = value
        eb[0, rows] = value.astype(jnp.bfloat16)
        pair_rows[q] = go(
            remote(eb.at[0, rows], eb.at[2, rows], s_zg.at[q], r_zg.at[q], pair_peer)
        )
        core_rows[q] = go(
            remote(eb.at[0, rows], eb.at[1, rows], s_cg.at[q], r_cg.at[q], core_peer)
        )
        if q == 1:
            with jax.named_scope("G_ids2"):
                id_copies[1].wait_recv()
                go(id_copies[2])
        if q == LAG:
            with jax.named_scope("G_ids3"):
                id_copies[0].wait_recv()
                id_copies[2].wait_recv()
            with jax.named_scope("G_mark"):
                for picks, cut in zip((picks0, picks1, picks2), cuts):
                    mark(picks, *cut)
        if q >= LAG:
            fetch(q - LAG)
        if q == n_seg - 2:
            with jax.named_scope("J_block0"):
                acc[...] = jnp.dot(
                    picks0[...], gathered(cuts[0]), preferred_element_type=jnp.float32
                )

    fetch(n_seg - LAG)
    with jax.named_scope("J_block1"):
        acc[...] += jnp.dot(picks1[...], gathered(cuts[1]), preferred_element_type=jnp.float32)
    for q in range(n_seg - LAG + 1, n_seg):
        fetch(q)
    with jax.named_scope("J_wait2"):
        last = gathered(cuts[2])

    group = nx * ny * CL_OWN
    order = [*range(1, nq), 0]
    a1, b1, a2, b2, zs = {}, {}, {}, {}, []
    for dz in order:
        rows = pl.ds(dz * group, group)
        with jax.named_scope("J_block2_%d" % dz):
            value = acc[rows] + jnp.dot(picks2[rows], last, preferred_element_type=jnp.float32)
            value = value.reshape(nx, ny, CL_OWN, width)
            for d in range(1, nx):
                sa[dz, d - 1] = value[d, :, :, :half].astype(jnp.bfloat16)
                a1[dz, d] = go(
                    remote(
                        sa.at[dz, d - 1], ra.at[dz, d - 1],
                        s_sa.at[dz, d - 1], r_sa.at[dz, d - 1], x_peer(d),
                    )
                )
            for d in range(1, ny):
                sb[dz, d - 1] = value[:, d, :, half:].astype(jnp.bfloat16)
                b1[dz, d] = go(
                    remote(
                        sb.at[dz, d - 1], rb.at[dz, d - 1],
                        s_sb.at[dz, d - 1], r_sb.at[dz, d - 1], y_peer(d),
                    )
                )
            oa[dz] = value[0, :, :, :half]
            ob[dz] = value[:, 0, :, half:]

    for dz in order:
        with jax.named_scope("L_wxa%d" % dz):
            for d in range(1, nx):
                a1[dz, d].wait_recv()
        for k in range(ny - 1, -1, -1):
            mine = oa[dz, k]
            for d in range(1, nx):
                mine += ra[dz, d - 1, k].astype(jnp.float32)
            if k:
                ya_s[dz, k - 1] = mine.astype(jnp.bfloat16)
                a2[dz, k] = go(
                    remote(
                        ya_s.at[dz, k - 1], ya_r.at[dz, k - 1],
                        s_ya.at[dz, k - 1], r_ya.at[dz, k - 1], y_peer(k),
                    )
                )
            else:
                fa[dz] = mine
        with jax.named_scope("L_wyb%d" % dz):
            for d in range(1, ny):
                b1[dz, d].wait_recv()
        for k in range(nx - 1, -1, -1):
            mine = ob[dz, k]
            for d in range(1, ny):
                mine += rb[dz, d - 1, k].astype(jnp.float32)
            if k:
                xb_s[dz, k - 1] = mine.astype(jnp.bfloat16)
                b2[dz, k] = go(
                    remote(
                        xb_s.at[dz, k - 1], xb_r.at[dz, k - 1],
                        s_xb.at[dz, k - 1], r_xb.at[dz, k - 1], x_peer(k),
                    )
                )
            else:
                fb[dz] = mine

    own = []
    for dz in order:
        for side, got, arrived, ahead, count, s_z, r_z in (
            (0, a2, ya_r, fa, ny, s_za, r_za),
            (1, b2, xb_r, fb, nx, s_zb, r_zb),
        ):
            with jax.named_scope("M_w%d_%d" % (dz, side)):
                for k in range(1, count):
                    got[dz, k].wait_recv()
            mine = ahead[dz]
            for k in range(1, count):
                mine += arrived[dz, k - 1].astype(jnp.float32)
            if dz:
                z_s[side, dz - 1] = mine.astype(jnp.bfloat16)
                zs.append(
                    go(
                        remote(
                            z_s.at[side, dz - 1], z_r.at[side, dz - 1],
                            s_z.at[dz - 1], r_z.at[dz - 1], z_peer(dz),
                        )
                    )
                )
            else:
                own.append(mine)
    with jax.named_scope("N_wz"):
        for copy in zs:
            copy.wait_recv()
    with jax.named_scope("O_fin"):
        for side in range(2):
            for d in range(1, nq):
                own[side] += z_r[side, d - 1].astype(jnp.float32)
        cen_ref[...] = unit_rows(jnp.concatenate(own, axis=1))

    with jax.named_scope("P_wsend"):
        for copy in sent:
            copy.wait_send()


def write_out(emb, cen, emb_out, cen_out, sem):
    copies = [
        pltpu.make_async_copy(emb, emb_out, sem.at[0]),
        pltpu.make_async_copy(cen, cen_out, sem.at[1]),
    ]
    for copy in copies:
        copy.start()
    for copy in copies:
        copy.wait()


def shards(features, tile_rows, tile_labels, tile_values, cluster_ids):
    n_tiles, tile = tile_values.shape[:2]
    width = features.shape[1]
    labels = cluster_ids.shape[0]
    n_inst, n_lab = lax.axis_size("inst"), lax.axis_size("lab")
    nx = n_inst // 2
    ny = nx if n_lab % nx == 0 else 1
    nz = n_lab // ny
    assert labels == tile and nz % PAIR == 0
    nq = nz // PAIR
    half = width // 2
    bf, f32 = jnp.bfloat16, jnp.float32
    ox, oy, oq = max(nx - 1, 1), max(ny - 1, 1), max(nq - 1, 1)
    segs, cuts = len(segments(tile)), blocks(tile)
    dma = lambda *shape: [pltpu.SemaphoreType.DMA(shape)] * 2
    vmem = pl.BlockSpec(memory_space=pltpu.VMEM)
    hbm = pl.BlockSpec(memory_space=pl.ANY)
    sums = nq * nx * ny * CL_OWN
    emb, cen = pl.pallas_call(
        functools.partial(kernel, nx, ny, nz),
        out_shape=(
            pltpu.VMEM((labels, width), f32),
            pltpu.VMEM((CL_OWN, width), f32),
        ),
        in_specs=[hbm] * 5,
        out_specs=(vmem, vmem),
        scratch_shapes=[
            pltpu.SMEM((n_tiles,), jnp.int32),
            pltpu.SMEM((n_tiles,), jnp.int32),
            pltpu.VMEM(features.shape, bf),
            pltpu.VMEM(tile_values.shape, bf),
            pltpu.VMEM(features.shape, bf),
            pltpu.VMEM((n_tiles + 1, tile, tile), bf),
            pltpu.VMEM((nx, tile, width), bf),
            pltpu.VMEM((nx, tile, width), bf),
            pltpu.VMEM((ox, tile, width), bf),
            pltpu.VMEM((ox, tile, width), bf),
            pltpu.VMEM((tile, width), f32),
            pltpu.VMEM((2 * PAIR, tile, width), bf),
            pltpu.VMEM((2 * PAIR, 1, tile), jnp.int32),
            *[pltpu.VMEM((sums, 2 * PAIR * (high - low)), bf) for low, high in cuts],
            pltpu.VMEM((sums, width), f32),
            pltpu.VMEM((nq, ox, ny, CL_OWN, half), bf),
            pltpu.VMEM((nq, ox, ny, CL_OWN, half), bf),
            pltpu.VMEM((nq, ny, CL_OWN, half), f32),
            pltpu.VMEM((nq, oy, nx, CL_OWN, half), bf),
            pltpu.VMEM((nq, oy, nx, CL_OWN, half), bf),
            pltpu.VMEM((nq, nx, CL_OWN, half), f32),
            pltpu.VMEM((nq, oy, CL_OWN, half), bf),
            pltpu.VMEM((nq, oy, CL_OWN, half), bf),
            pltpu.VMEM((nq, CL_OWN, half), f32),
            pltpu.VMEM((nq, ox, CL_OWN, half), bf),
            pltpu.VMEM((nq, ox, CL_OWN, half), bf),
            pltpu.VMEM((nq, CL_OWN, half), f32),
            pltpu.VMEM((2, oq, CL_OWN, half), bf),
            pltpu.VMEM((2, oq, CL_OWN, half), bf),
            pltpu.SemaphoreType.DMA((3,)),
            pltpu.SemaphoreType.DMA((n_tiles,)),
            pltpu.SemaphoreType.DMA((features.shape[0] // tile,)),
            *dma(nx, segs),
            *dma(ox, segs),
            *dma(segs),
            *dma(segs),
            *dma(segs),
            *dma(3),
            *dma(nq, ox),
            *dma(nq, oy),
            *dma(nq, oy),
            *dma(nq, ox),
            *dma(oq),
            *dma(oq),
        ],
        compiler_params=pltpu.CompilerParams(
            collective_id=0, has_side_effects=True, vmem_limit_bytes=60 * 1024 * 1024
        ),
        name="pifa_step",
    )(tile_rows, tile_labels, cluster_ids.reshape(1, labels), features, tile_values)
    return pl.pallas_call(
        write_out,
        out_shape=(
            jax.ShapeDtypeStruct((labels, width), f32),
            jax.ShapeDtypeStruct((CL_OWN, width), f32),
        ),
        in_specs=[vmem, vmem],
        out_specs=(hbm, hbm),
        scratch_shapes=[pltpu.SemaphoreType.DMA((2,))],
        name="write_out",
    )(
        pltpu.with_memory_space_constraint(emb, pltpu.VMEM),
        pltpu.with_memory_space_constraint(cen, pltpu.VMEM),
    )


def solution(mesh):
    return jax.shard_map(
        shards,
        mesh=mesh,
        in_specs=(
            P("inst", None),
            P(("inst", "lab")),
            P(("inst", "lab")),
            P(("inst", "lab"), None, None),
            P(("lab", "inst")),
        ),
        out_specs=(P(("lab", "inst"), None), P(("inst", "lab"), None)),
        check_vma=False,
    )
```

profile of v0, /device:TPU:0, one launch (start us, length us, event | category | flops | bytes accessed | tf_op | source)
XLA Modules:
  0.0 35.0 jit_solution(3760133711357482613)
XLA Ops:
  0.6 33.5 %pifa_step.1 = (f32[256,768]{1,0:T(8,128)S(1)}, f32[32,768]{1,0:T(8,128)S(1)}) custom-call(s32[4]{0:T(128)} %rows_hbm.1, s32[4]{0:T(128)} %labs_hbm.1, s32[1,256]{1,0:T(1,128)} %bitcast.1, bf16[512,768]{1,0:T(8,128)(2,1)} %feat_hbm.1, bf16[4,256,256]{2,1,0:T(8,128)(2,1)} %val_hbm.1), custom_call_target="tpu_custom_call" | custom-call | tf_op jit(solution)/shard_map/pifa_step/pallas_call | solution.py:388
  34.1 0.9 %write_out.1 = (f32[256,768]{1,0:T(8,128)}, f32[32,768]{1,0:T(8,128)}) custom-call(f32[256,768]{1,0:T(8,128)S(1)} %get-tuple-element.4.emb, f32[32,768]{1,0:T(8,128)S(1)} %get-tuple-element.5.cen), custom_call_target="tpu_custom_call" | custom-call | tf_op jit(solution)/shard_map/write_out/pallas_call | solution.py:447
where the time goes:
time: 35.2 us; the launch traced here: 35 us
  Pallas kernels  34.4 us (98%)
  between operations  0.64 us (2%)
    pallas_call x1, Pallas kernels, shards(): pl.pallas_call(functools.partial(kernel, nx, ny, nz), out_shape=(pltpu.VM...  33.5 us
    pallas_call x1, Pallas kernels, shards(): pl.pallas_call(write_out, out_shape=(jax.ShapeDtypeStruct((labels, width)...  0.92 us

commit v1 on v0

--- a/solution.py
+++ b/solution.py
@@ -9,7 +9,9 @@
 
 CL_OWN = 32
 PAIR = 2
-LAG = 3
+LAG = 4
+DIRECT = 1
+SPLIT = 2
 MESH = pl.DeviceIdType.MESH
 
 
@@ -50,6 +52,7 @@
     segs = segments(tile)
     cuts = blocks(tile)
     n_seg = len(segs)
+    part = CL_OWN // SPLIT
 
     x_at = lambda d: (x + d) % nx
     y_at = lambda d: (y + d) % ny
@@ -65,7 +68,8 @@
     peers += [x_peer(d) for d in range(1, nx)]
     peers += [y_peer(d) for d in range(1, ny)]
     peers += [z_peer(d) for d in range(1, nq)]
-    peers.append(pair_peer)
+    diag_peer = (x * 2 + other, pair_peer[1])
+    peers += [diag_peer, pair_peer]
 
     barrier = pltpu.get_barrier_semaphore()
     for peer in peers:
@@ -182,22 +186,25 @@
     def mark(picks, low, high):
         near = jnp.concatenate([ids[s, :, low:high] for s in range(2 * PAIR)], axis=1)
         count = 2 * PAIR * (high - low)
-        near = jnp.broadcast_to(near, (CL_OWN, count))
-        step = lax.broadcasted_iota(jnp.int32, (CL_OWN, count), 0)
+        near = jnp.broadcast_to(near, (part, count))
+        step = lax.broadcasted_iota(jnp.int32, (part, count), 0)
         row = 0
         for dz in range(nq):
-            for dx in range(nx):
-                for dy in range(ny):
-                    owner = (x_at(dx) * 2 + c) * nz + zq_at(dz) * PAIR + zr
-                    base = (owner * ny + y_at(dy)) * CL_OWN
-                    hit = jnp.where(near == step + base, 1.0, 0.0)
-                    picks[pl.ds(row, CL_OWN)] = hit.astype(jnp.bfloat16)
-                    row += CL_OWN
+            for g in range(SPLIT):
+                for dx in range(nx):
+                    for dy in range(ny):
+                        owner = (x_at(dx) * 2 + c) * nz + zq_at(dz) * PAIR + zr
+                        base = (owner * ny + y_at(dy)) * CL_OWN + g * part
+                        hit = jnp.where(near == step + base, 1.0, 0.0)
+                        picks[pl.ds(row, part)] = hit.astype(jnp.bfloat16)
+                        row += part
 
     pair_rows, core_rows, passed = {}, {}, {}
 
     def fetch(q):
         rows = pl.ds(*segs[q])
+        if q >= n_seg - DIRECT:
+            return
         with jax.named_scope("I_fetch%d" % q):
             pair_rows[q].wait_recv()
         passed[q] = go(
@@ -207,6 +214,8 @@
     def gathered(cut):
         for q, (first, _) in enumerate(segs):
             if cut[0] <= first < cut[1]:
+                if q >= n_seg - DIRECT:
+                    pair_rows[q].wait_recv()
                 core_rows[q].wait_recv()
                 passed[q].wait_recv()
         return eb[:, cut[0] : cut[1]].reshape(2 * PAIR * (cut[1] - cut[0]), width)
@@ -225,6 +234,10 @@
         pair_rows[q] = go(
             remote(eb.at[0, rows], eb.at[2, rows], s_zg.at[q], r_zg.at[q], pair_peer)
         )
+        if q >= n_seg - DIRECT:
+            passed[q] = go(
+                remote(eb.at[0, rows], eb.at[3, rows], s_fw.at[q], r_fw.at[q], diag_peer)
+            )
         core_rows[q] = go(
             remote(eb.at[0, rows], eb.at[1, rows], s_cg.at[q], r_cg.at[q], core_peer)
         )
@@ -241,115 +254,140 @@
                     mark(picks, *cut)
         if q >= LAG:
             fetch(q - LAG)
+
+    for q in range(n_seg - LAG, n_seg):
         if q == n_seg - 2:
             with jax.named_scope("J_block0"):
                 acc[...] = jnp.dot(
                     picks0[...], gathered(cuts[0]), preferred_element_type=jnp.float32
                 )
-
-    fetch(n_seg - LAG)
+        fetch(q)
     with jax.named_scope("J_block1"):
         acc[...] += jnp.dot(picks1[...], gathered(cuts[1]), preferred_element_type=jnp.float32)
-    for q in range(n_seg - LAG + 1, n_seg):
-        fetch(q)
     with jax.named_scope("J_wait2"):
         last = gathered(cuts[2])
 
     group = nx * ny * CL_OWN
-    order = [*range(1, nq), 0]
+    far = [(dz, g) for dz in range(1, nq) for g in range(SPLIT)]
+    home = [(0, g) for g in range(SPLIT)]
     a1, b1, a2, b2, zs = {}, {}, {}, {}, []
-    for dz in order:
+
+    def local(dz):
         rows = pl.ds(dz * group, group)
-        with jax.named_scope("J_block2_%d" % dz):
-            value = acc[rows] + jnp.dot(picks2[rows], last, preferred_element_type=jnp.float32)
-            value = value.reshape(nx, ny, CL_OWN, width)
+        value = acc[rows] + jnp.dot(picks2[rows], last, preferred_element_type=jnp.float32)
+        value = value.reshape(SPLIT, nx, ny, part, width)
+        for g in range(SPLIT):
+            at = dz * SPLIT + g
             for d in range(1, nx):
-                sa[dz, d - 1] = value[d, :, :, :half].astype(jnp.bfloat16)
-                a1[dz, d] = go(
+                sa[at, d - 1] = value[g, d, :, :, :half].astype(jnp.bfloat16)
+            for d in range(1, ny):
+                sb[at, d - 1] = value[g, :, d, :, half:].astype(jnp.bfloat16)
+            oa[at] = value[g, 0, :, :, :half]
+            ob[at] = value[g, :, 0, :, half:]
+
+    def first(dz, g):
+        at = dz * SPLIT + g
+        for d in range(1, nx):
+            a1[dz, g, d] = go(
+                remote(
+                    sa.at[at, d - 1], ra.at[at, d - 1],
+                    s_sa.at[at, d - 1], r_sa.at[at, d - 1], x_peer(d),
+                )
+            )
+        for d in range(1, ny):
+            b1[dz, g, d] = go(
+                remote(
+                    sb.at[at, d - 1], rb.at[at, d - 1],
+                    s_sb.at[at, d - 1], r_sb.at[at, d - 1], y_peer(d),
+                )
+            )
+
+    def second(dz, g):
+        at = dz * SPLIT + g
+        with jax.named_scope("L_wa%d%d" % (dz, g)):
+            for d in range(1, nx):
+                a1[dz, g, d].wait_recv()
+        for k in range(ny - 1, -1, -1):
+            mine = oa[at, k]
+            for d in range(1, nx):
+                mine += ra[at, d - 1, k].astype(jnp.float32)
+            if k:
+                ya_s[at, k - 1] = mine.astype(jnp.bfloat16)
+                a2[dz, g, k] = go(
                     remote(
-                        sa.at[dz, d - 1], ra.at[dz, d - 1],
-                        s_sa.at[dz, d - 1], r_sa.at[dz, d - 1], x_peer(d),
+                        ya_s.at[at, k - 1], ya_r.at[at, k - 1],
+                        s_ya.at[at, k - 1], r_ya.at[at, k - 1], y_peer(k),
                     )
                 )
+            else:
+                fa[at] = mine
+        with jax.named_scope("L_wb%d%d" % (dz, g)):
             for d in range(1, ny):
-                sb[dz, d - 1] = value[:, d, :, half:].astype(jnp.bfloat16)
-                b1[dz, d] = go(
+                b1[dz, g, d].wait_recv()
+        for k in range(nx - 1, -1, -1):
+            mine = ob[at, k]
+            for d in range(1, ny):
+                mine += rb[at, d - 1, k].astype(jnp.float32)
+            if k:
+                xb_s[at, k - 1] = mine.astype(jnp.bfloat16)
+                b2[dz, g, k] = go(
                     remote(
-                        sb.at[dz, d - 1], rb.at[dz, d - 1],
-                        s_sb.at[dz, d - 1], r_sb.at[dz, d - 1], y_peer(d),
+                        xb_s.at[at, k - 1], xb_r.at[at, k - 1],
+                        s_xb.at[at, k - 1], r_xb.at[at, k - 1], x_peer(k),
                     )
                 )
-            oa[dz] = value[0, :, :, :half]
-            ob[dz] = value[:, 0, :, half:]
-
-    for dz in order:
-        with jax.named_scope("L_wxa%d" % dz):
-            for d in range(1, nx):
-                a1[dz, d].wait_recv()
-        for k in range(ny - 1, -1, -1):
-            mine = oa[dz, k]
-            for d in range(1, nx):
-                mine += ra[dz, d - 1, k].astype(jnp.float32)
-            if k:
-                ya_s[dz, k - 1] = mine.astype(jnp.bfloat16)
-                a2[dz, k] = go(
-                    remote(
-                        ya_s.at[dz, k - 1], ya_r.at[dz, k - 1],
-                        s_ya.at[dz, k - 1], r_ya.at[dz, k - 1], y_peer(k),
-                    )
-                )
             else:
-                fa[dz] = mine
-        with jax.named_scope("L_wyb%d" % dz):
-            for d in range(1, ny):
-                b1[dz, d].wait_recv()
-        for k in range(nx - 1, -1, -1):
-            mine = ob[dz, k]
-            for d in range(1, ny):
-                mine += rb[dz, d - 1, k].astype(jnp.float32)
-            if k:
-                xb_s[dz, k - 1] = mine.astype(jnp.bfloat16)
-                b2[dz, k] = go(
-                    remote(
-                        xb_s.at[dz, k - 1], xb_r.at[dz, k - 1],
-                        s_xb.at[dz, k - 1], r_xb.at[dz, k - 1], x_peer(k),
-                    )
-                )
-            else:
-                fb[dz] = mine
-
-    own = []
-    for dz in order:
+                fb[at] = mine
+
+    def third(dz, g):
+        at = dz * SPLIT + g
+        done = []
         for side, got, arrived, ahead, count, s_z, r_z in (
             (0, a2, ya_r, fa, ny, s_za, r_za),
             (1, b2, xb_r, fb, nx, s_zb, r_zb),
         ):
-            with jax.named_scope("M_w%d_%d" % (dz, side)):
+            with jax.named_scope("M_w%d%d_%d" % (dz, g, side)):
                 for k in range(1, count):
-                    got[dz, k].wait_recv()
-            mine = ahead[dz]
+                    got[dz, g, k].wait_recv()
+            mine = ahead[at]
             for k in range(1, count):
-                mine += arrived[dz, k - 1].astype(jnp.float32)
+                mine += arrived[at, k - 1].astype(jnp.float32)
             if dz:
-                z_s[side, dz - 1] = mine.astype(jnp.bfloat16)
-                zs.append(
-                    go(
-                        remote(
-                            z_s.at[side, dz - 1], z_r.at[side, dz - 1],
-                            s_z.at[dz - 1], r_z.at[dz - 1], z_peer(dz),
-                        )
-                    )
-                )
-            else:
-                own.append(mine)
+                to = at - SPLIT
+                z_s[side, to] = mine.astype(jnp.bfloat16)
+                copy = remote(
+                    z_s.at[side, to], z_r.at[side, to],
+                    s_z.at[to], r_z.at[to], z_peer(dz),
+                )
+                zs.append(go(copy))
+            done.append(mine)
+        return done
+
+    for dz in range(1, nq):
+        with jax.named_scope("J_block2_%d" % dz):
+            local(dz)
+            for g in range(SPLIT):
+                first(dz, g)
+    with jax.named_scope("J_block2_0"):
+        local(0)
+    for piece in far:
+        second(*piece)
+    for piece in home:
+        first(*piece)
+    for piece in far:
+        third(*piece)
+    for piece in home:
+        second(*piece)
+    own = [third(*piece) for piece in home]
     with jax.named_scope("N_wz"):
         for copy in zs:
             copy.wait_recv()
     with jax.named_scope("O_fin"):
-        for side in range(2):
-            for d in range(1, nq):
-                own[side] += z_r[side, d - 1].astype(jnp.float32)
-        cen_ref[...] = unit_rows(jnp.concatenate(own, axis=1))
+        for g in range(SPLIT):
+            for side in range(2):
+                for d in range(1, nq):
+                    own[g][side] += z_r[side, (d - 1) * SPLIT + g].astype(jnp.float32)
+            cen_ref[pl.ds(g * part, part)] = unit_rows(jnp.concatenate(own[g], axis=1))
 
     with jax.named_scope("P_wsend"):
         for copy in sent:
@@ -384,6 +422,7 @@
     dma = lambda *shape: [pltpu.SemaphoreType.DMA(shape)] * 2
     vmem = pl.BlockSpec(memory_space=pltpu.VMEM)
     hbm = pl.BlockSpec(memory_space=pl.ANY)
+    part = CL_OWN // SPLIT
     sums = nq * nx * ny * CL_OWN
     emb, cen = pl.pallas_call(
         functools.partial(kernel, nx, ny, nz),
@@ -409,20 +448,20 @@
             pltpu.VMEM((2 * PAIR, 1, tile), jnp.int32),
             *[pltpu.VMEM((sums, 2 * PAIR * (high - low)), bf) for low, high in cuts],
             pltpu.VMEM((sums, width), f32),
-            pltpu.VMEM((nq, ox, ny, CL_OWN, half), bf),
-            pltpu.VMEM((nq, ox, ny, CL_OWN, half), bf),
-            pltpu.VMEM((nq, ny, CL_OWN, half), f32),
-            pltpu.VMEM((nq, oy, nx, CL_OWN, half), bf),
-            pltpu.VMEM((nq, oy, nx, CL_OWN, half), bf),
-            pltpu.VMEM((nq, nx, CL_OWN, half), f32),
-            pltpu.VMEM((nq, oy, CL_OWN, half), bf),
-            pltpu.VMEM((nq, oy, CL_OWN, half), bf),
-            pltpu.VMEM((nq, CL_OWN, half), f32),
-            pltpu.VMEM((nq, ox, CL_OWN, half), bf),
-            pltpu.VMEM((nq, ox, CL_OWN, half), bf),
-            pltpu.VMEM((nq, CL_OWN, half), f32),
-            pltpu.VMEM((2, oq, CL_OWN, half), bf),
-            pltpu.VMEM((2, oq, CL_OWN, half), bf),
+            pltpu.VMEM((nq * SPLIT, ox, ny, part, half), bf),
+            pltpu.VMEM((nq * SPLIT, ox, ny, part, half), bf),
+            pltpu.VMEM((nq * SPLIT, ny, part, half), f32),
+            pltpu.VMEM((nq * SPLIT, oy, nx, part, half), bf),
+            pltpu.VMEM((nq * SPLIT, oy, nx, part, half), bf),
+            pltpu.VMEM((nq * SPLIT, nx, part, half), f32),
+            pltpu.VMEM((nq * SPLIT, oy, part, half), bf),
+            pltpu.VMEM((nq * SPLIT, oy, part, half), bf),
+            pltpu.VMEM((nq * SPLIT, part, half), f32),
+            pltpu.VMEM((nq * SPLIT, ox, part, half), bf),
+            pltpu.VMEM((nq * SPLIT, ox, part, half), bf),
+            pltpu.VMEM((nq * SPLIT, part, half), f32),
+            pltpu.VMEM((2, oq * SPLIT, part, half), bf),
+            pltpu.VMEM((2, oq * SPLIT, part, half), bf),
             pltpu.SemaphoreType.DMA((3,)),
             pltpu.SemaphoreType.DMA((n_tiles,)),
             pltpu.SemaphoreType.DMA((features.shape[0] // tile,)),
@@ -432,12 +471,12 @@
             *dma(segs),
             *dma(segs),
             *dma(3),
-            *dma(nq, ox),
-            *dma(nq, oy),
-            *dma(nq, oy),
-            *dma(nq, ox),
-            *dma(oq),
-            *dma(oq),
+            *dma(nq * SPLIT, ox),
+            *dma(nq * SPLIT, oy),
+            *dma(nq * SPLIT, oy),
+            *dma(nq * SPLIT, ox),
+            *dma(oq * SPLIT),
+            *dma(oq * SPLIT),
         ],
         compiler_params=pltpu.CompilerParams(
             collective_id=0, has_side_effects=True, vmem_limit_bytes=60 * 1024 * 1024

time: 35.2 us -> 34.4 us (0.977)
  Pallas kernels: 34.4 us -> 33.7 us
    pallas_call x1, Pallas kernels: 33.5 us -> 32.7 us  [shards(): pl.pallas_call(functools.partial(kernel, nx, ny, nz), out_shape=(pltpu.VM...]
where the time goes in v1:
time: 34.4 us; the launch traced here: 34.3 us
  Pallas kernels  33.7 us (98%)
  between operations  0.64 us (2%)
    pallas_call x1, Pallas kernels, shards(): pl.pallas_call(functools.partial(kernel, nx, ny, nz), out_shape=(pltpu.VM...  32.7 us
    pallas_call x1, Pallas kernels, shards(): pl.pallas_call(write_out, out_shape=(jax.ShapeDtypeStruct((labels, width)...  0.92 us

profile of v1, /device:TPU:0, one launch (start us, length us, event | category | flops | bytes accessed | tf_op | source)
XLA Modules:
  0.0 34.3 jit_solution(922032835465579764)
XLA Ops:
  0.6 32.7 %pifa_step.1 = (f32[256,768]{1,0:T(8,128)S(1)}, f32[32,768]{1,0:T(8,128)S(1)}) custom-call(s32[4]{0:T(128)} %rows_hbm.1, s32[4]{0:T(128)} %labs_hbm.1, s32[1,256]{1,0:T(1,128)} %bitcast.1, bf16[512,768]{1,0:T(8,128)(2,1)} %feat_hbm.1, bf16[4,256,256]{2,1,0:T(8,128)(2,1)} %val_hbm.1), custom_call_target="tpu_custom_call" | custom-call | tf_op jit(solution)/shard_map/pifa_step/pallas_call | solution.py:427
  33.4 0.9 %write_out.1 = (f32[256,768]{1,0:T(8,128)}, f32[32,768]{1,0:T(8,128)}) custom-call(f32[256,768]{1,0:T(8,128)S(1)} %get-tuple-element.4.emb, f32[32,768]{1,0:T(8,128)S(1)} %get-tuple-element.5.cen), custom_call_target="tpu_custom_call" | custom-call | tf_op jit(solution)/shard_map/write_out/pallas_call | solution.py:486
